TPU v7x, 32 devices: a whole 2x2x4 slice. The times are simulated.
32 devices in a mesh: seq: 4 (over y, core), batch: 8 (over z, x).
Axes of the slice: x: 2, y: 2, z: 4, core: 2. Of those that a mesh axis runs over, the one named last changes fastest.
Arguments:
- waveforms: bfloat16 [8, 24, 16000], P('batch', 'seq'), may hold values from -6 to 6
- clip_lengths: int32 [8, 4], P('batch'), may hold values from 1 to 6, as said below
- block_starts: int32 [8, 24], P('batch'), may hold values from 0 to 744, as said below
- conv_first: bfloat16 [384, 1280], P('batch'), may hold values from -0.3125 to 0.3125
- bias_first: float32 [1280], replicated, may hold values from -3 to 3
- conv_second: bfloat16 [3840, 1280], replicated, may hold values from -0.09375 to 0.09375
- bias_second: float32 [1280], replicated, may hold values from -3 to 3
- norm_gain: float32 [1280], replicated, may hold values from 0.25 to 1.75
- projector: bfloat16 [1280, 4096], P(None, 'seq'), may hold values from -0.15625 to 0.15625
- proj_bias: float32 [4096], P('seq'), may hold values from -3 to 3
Outputs:
- audio_rows: bfloat16 [8, 768, 4096], P('batch', 'seq')
Inputs may be any that keep to these rules, and one draw needn't show every extreme that they name: `clip_lengths`: the lengths of a sequence's 4 clips sum to 12, and one clip has 6 blocks. `block_starts`: A clip's live blocks start 24 positions apart, in slot order; live blocks of a sequence occupy disjoint positions; entries of dead slots are 0.
All inputs are finite; a program needn't handle non-finite values.
Results may differ from a plain program's by a relative error of at most 0.0055.
Values may be sent and summed in bfloat16 or wider, within the bound.
A program may use at most 64 MiB of HBM per device.

v0:
```python
import jax
import jax.numpy as jnp
import numpy as np
from jax import lax
from jax.sharding import PartitionSpec as P

MEL = 128
WIDTH = 1280
HOP = 160
WINDOW = 400
BINS = 201
FRAMES = 96
TOK = 24
OWN_ROWS = 192


def hertz_to_mel(hertz):
    return np.where(
        hertz < 1000.0,
        hertz / (200.0 / 3.0),
        15.0 + np.log(np.maximum(hertz, 1.0) / 1000.0) / (np.log(6.4) / 27.0),
    )


def mel_to_hertz(mels):
    return np.where(
        mels < 15.0, mels * 200.0 / 3.0, 1000.0 * np.exp((mels - 15.0) * np.log(6.4) / 27.0)
    )


def spectral_tables():
    sample_rate = HOP * 100.0
    sample_index = np.arange(WINDOW)
    hann = 0.5 - 0.5 * np.cos(2.0 * np.pi * sample_index / WINDOW)
    angles = 2.0 * np.pi * np.outer(sample_index, np.arange(BINS)) / WINDOW
    dft_basis = np.concatenate(
        [hann[:, None] * np.cos(angles), -hann[:, None] * np.sin(angles)], axis=1
    )
    edges = mel_to_hertz(
        np.linspace(0.0, float(hertz_to_mel(np.array(sample_rate / 2.0))), MEL + 2)
    )
    bin_hertz = np.arange(BINS) * sample_rate / WINDOW
    rising = (bin_hertz[:, None] - edges[None, :-2]) / (edges[1:-1] - edges[:-2])[None, :]
    falling = (edges[None, 2:] - bin_hertz[:, None]) / (edges[2:] - edges[1:-1])[None, :]
    filters = (
        np.maximum(0.0, np.minimum(rising, falling)) * (2.0 / (edges[2:] - edges[:-2]))[None, :]
    )
    return (jnp.asarray(dft_basis.astype(np.float32)), jnp.asarray(filters.astype(np.float32)))


def encode(blocks_in, tables, conv_first, bias_first, conv_second, bias_second, norm_gain):
    dft_basis, filters = tables
    block_count = blocks_in.shape[0]
    segments = blocks_in.astype(jnp.float32).reshape(block_count, FRAMES + 4, HOP)
    frames = jnp.concatenate(
        [
            segments[:, :FRAMES],
            segments[:, 1 : FRAMES + 1],
            segments[:, 2 : FRAMES + 2, : HOP // 2],
        ],
        axis=2,
    )
    frames = frames.reshape(block_count * FRAMES, WINDOW)
    spectrum = jnp.dot(frames, dft_basis, precision=lax.Precision.HIGHEST)
    power_bins = spectrum[:, :BINS] * spectrum[:, :BINS] + spectrum[:, BINS:] * spectrum[:, BINS:]
    energy = jnp.dot(power_bins, filters, precision=lax.Precision.HIGHEST)
    features = (
        ((jnp.log10(energy + 1e-10) + 4.0) / 4.0)
        .astype(jnp.bfloat16)
        .reshape(block_count, FRAMES, MEL)
    )
    zero_mel = jnp.zeros((block_count, 1, MEL), jnp.bfloat16)
    padded = jnp.concatenate([zero_mel, features, zero_mel], axis=1)
    stacked = jnp.concatenate([padded[:, :-2], padded[:, 1:-1], padded[:, 2:]], axis=2).reshape(
        block_count * FRAMES, 3 * MEL
    )
    hidden = jax.nn.gelu(
        jnp.dot(stacked, conv_first, preferred_element_type=jnp.float32) + bias_first,
        approximate=False,
    )
    hidden = hidden.astype(jnp.bfloat16).reshape(block_count, FRAMES // 2, 2, WIDTH)
    even_rows = hidden[:, :, 0]
    odd_rows = hidden[:, :, 1]
    before = jnp.concatenate(
        [jnp.zeros((block_count, 1, WIDTH), jnp.bfloat16), odd_rows[:, :-1]], axis=1
    )
    second_in = jnp.concatenate([before, even_rows, odd_rows], axis=2).reshape(
        block_count * FRAMES // 2, 3 * WIDTH
    )
    activated = jax.nn.gelu(
        jnp.dot(second_in, conv_second, preferred_element_type=jnp.float32) + bias_second,
        approximate=False,
    )
    pooled = jnp.mean(activated.reshape(block_count, TOK, 2, WIDTH), axis=2)
    row_mean = jnp.mean(pooled, axis=-1, keepdims=True)
    centred = pooled - row_mean
    row_var = jnp.mean(centred * centred, axis=-1, keepdims=True)
    normed = centred / jnp.sqrt(row_var + 1e-05) * norm_gain
    return normed.astype(jnp.bfloat16).reshape(block_count * TOK, WIDTH)


def shards(
    waveforms,
    clip_lengths,
    block_starts,
    conv_first,
    bias_first,
    conv_second,
    bias_second,
    norm_gain,
    projector,
    proj_bias,
):
    tables = spectral_tables()
    devices_seq = lax.axis_size("seq")
    slots_all = waveforms.shape[1]
    lengths = clip_lengths[0]
    starts = block_starts[0]
    whole_first = lax.all_gather(conv_first, "batch", axis=0, tiled=True)
    blocks = waveforms[0]
    group_slot = jnp.arange(devices_seq * slots_all, dtype=jnp.int32)
    group_live = group_slot % slots_all < jnp.repeat(lengths, slots_all)
    token_rows = encode(
        blocks, tables, whole_first, bias_first, conv_second, bias_second, norm_gain
    )
    projected = (
        jnp.dot(
            lax.all_gather(token_rows, "seq", axis=0, tiled=True),
            projector,
            preferred_element_type=jnp.float32,
        )
        + proj_bias
    ).astype(jnp.bfloat16)
    total_rows = projected.shape[0]
    length_all = devices_seq * OWN_ROWS
    offsets = jnp.arange(TOK, dtype=jnp.int32)
    target = jnp.where(group_live[:, None], starts[:, None] + offsets[None, :], length_all).reshape(
        -1
    )
    row_index = (
        jnp.full((length_all,), total_rows, jnp.int32)
        .at[target]
        .set(jnp.arange(total_rows, dtype=jnp.int32), mode="drop")
    )
    padded_rows = jnp.concatenate(
        [projected, jnp.zeros((1, projected.shape[1]), jnp.bfloat16)], axis=0
    )
    placed = jnp.take(padded_rows, row_index, axis=0)
    owned_rows = lax.all_to_all(placed, "seq", split_axis=0, concat_axis=1, tiled=True)
    return owned_rows[None]


def solution(mesh):
    return jax.shard_map(
        shards,
        mesh=mesh,
        in_specs=(
            P("batch", "seq", None),
            P("batch", None),
            P("batch", None),
            P("batch", None),
            P(),
            P(),
            P(),
            P(),
            P(None, "seq"),
            P("seq"),
        ),
        out_specs=P("batch", "seq", None),
        check_vma=False,
    )
```

profile of v0, /device:TPU:0, one launch (start us, length us, event | category | flops | bytes accessed | tf_op | source)
XLA Modules:
  0.0 152.7 jit_solution(5425280199517510005)
XLA Ops:
  6.5 1.5 reshape.141
  8.0 0.1 fusion.49
  8.1 0.0 copy-start.1
  8.2 0.5 pad_maximum_fusion
  8.6 0.0 copy-start.9
  8.6 0.6 copy-done.1
  9.3 2.4 %fusion.50 = f32[576,402]{0,1:T(8,128)S(1)} fusion(f32[576,400]{1,0:T(8,128)S(1)} %bitcast.32, f32[400,402]{1,0:T(8,128)S(1)} %copy-done.1), kind=kOutput, calls=%fused_computation.88 | convolution fusion | flops 1111449600 | bytes 2491008 | tf_op jit(solution)/shard_map/dot_general | solution.py:64
  11.7 0.0 copy-start.2
  11.7 0.0 copy-start.6
  11.7 1.2 fusion.30
  12.9 0.1 pad_slice_fusion.1
  13.0 34.7 %all_gather.6 = bf16[384,1280]{1,0:T(8,128)(2,1)S(1)} all-gather(bf16[48,1280]{1,0:T(8,128)(2,1)S(1)} %copy-done.2), channel_id=1, replica_groups=mesh['seq'=4,'batch'=8] {'batch'}, dimensions={0}, use_global_device_ids=true | all-gather | bytes 1105920 | tf_op jit(solution)/shard_map/all_gather | solution.py:119
  47.7 7.8 %fusion.2 = bf16[576,1280]{1,0:T(8,128)(2,1)} fusion(bf16[384,1280]{1,0:T(8,128)(2,1)S(1)} %all_gather.6, f32[1280]{0:T(1024)S(1)} %copy-done.6, bf16[576,128]{1,0:T(8,128)(2,1)S(1)} %bitcast.39, bf16[576,128]{1,0:T(8,128)(2,1)S(1)} %fusion.30, bf16[576,128]{1,0:T(8,128)(2,1)S(1)} %bitcast.38), kind=kOutput, calls=%fused_computation.6 | convolution fusion | flops 616218624 | bytes 2905088 | tf_op jit(solution)/shard_map/dot_general | solution.py:78
  55.5 4.3 %reshape.139 = bf16[6,48,2,1280]{3,2,1,0:T(2,128)(2,1)} reshape(bf16[576,1280]{1,0:T(8,128)(2,1)} %fusion.2) | data formatting | bytes 2949120 | tf_op jit(solution)/shard_map/reshape | solution.py:81
  59.8 4.3 %fusion.48 = (bf16[6,48,1,1280]{3,2,1,0:T(2,128)(2,1)S(1)}, bf16[6,48,1,1280]{3,2,1,0:T(2,128)(2,1)S(1)}) fusion(bf16[6,48,2,1280]{3,2,1,0:T(2,128)(2,1)} %reshape.139), kind=kLoop, calls=%fused_computation.86 | loop fusion | bytes 2949120 | tf_op jit(solution)/shard_map/slice | solution.py:82
  64.1 0.1 copy.23
  64.2 0.1 copy.20
  64.3 0.0 copy-start.7
  64.3 0.1 copy.21
  64.4 0.2 concatenate.40
  64.6 0.4 copy-done.7
  65.0 10.8 %fusion.16 = f32[288,1280]{1,0:T(8,128)} fusion(bf16[3840,1280]{1,0:T(8,128)(2,1)} %param.17, bf16[288,1280]{1,0:T(8,128)(2,1)S(1)} %bitcast.34, bf16[288,1280]{1,0:T(8,128)(2,1)S(1)} %bitcast.35, bf16[288,1280]{1,0:T(8,128)(2,1)S(1)} %bitcast.36, f32[1280]{0:T(1024)S(1)} %copy-done.7), kind=kOutput, calls=%fused_computation.32 | convolution fusion | flops 2861752320 | bytes 13521920 | tf_op jit(solution)/shard_map/dot_general | solution.py:91
  75.9 3.0 %reshape.140 = f32[6,24,2,1280]{3,2,1,0:T(2,128)} reshape(f32[288,1280]{1,0:T(8,128)} %fusion.16) | data formatting | bytes 2949120 | tf_op jit(solution)/shard_map/reshape | solution.py:94
  78.9 3.1 %reduce_sum.27 = f32[6,24,1280]{2,1,0:T(8,128)S(1)} reduce(f32[6,24,2,1280]{3,2,1,0:T(2,128)} %reshape.140, f32[]{:T(128)} %constant.65.clone.1), dimensions={2}, to_apply=%region_1.2 | reduce | flops 184320 | bytes 2211844 | tf_op jit(solution)/shard_map/reduce_sum | solution.py:94
  82.0 0.0 copy-start.3
  82.0 0.1 fusion.47
  82.1 0.0 copy-start.4
  82.2 0.0 copy-start.5
  82.2 0.0 copy-start.8
  82.2 0.9 multiply_reduce_fusion
  83.1 0.1 div.33
  83.2 0.1 sqrt.12
  83.3 2.0 %fusion.33 = bf16[144,1280]{1,0:T(8,128)(2,1)} fusion(f32[6,24,1280]{2,1,0:T(8,128)} %get-tuple-element.8, f32[1280]{0:T(1024)S(1)} %copy-done.3, f32[144]{0:T(256)S(1)} %sqrt.12, f32[144]{0:T(256)S(1)} %div.33), kind=kLoop, calls=%fused_computation.58 | loop fusion | flops 737280 | bytes 1112192 | tf_op jit(solution)/shard_map/convert_element_type | solution.py:99
  85.3 0.0 all-gather.2.cloned.1.call-update
  85.3 0.1 broadcast_in_dim.50
  85.4 0.1 reshape.136
  85.5 0.1 add_select_fusion
  85.6 0.1 select_n.48
  85.7 4.1 %scatter_custom_fusion = s32[768]{0:T(1024)S(1)} fusion(s32[576]{0:T(1024)S(1)} %fusion.41, s32[576]{0:T(1024)S(1)} %iota.13, s32[]{:T(128)} %constant.45.clone.1), kind=kCustom, calls=%fused_computation.79 | custom fusion | bytes 3076 | tf_op jit(solution)/shard_map/scatter | solution.py:143
  89.8 0.1 broadcast_in_dim.54
  89.9 15.4 %all-gather.2.cloned.1.call-done = bf16[576,1280]{1,0:T(8,128)(2,1)} async-done(((bf16[144,1280]{1,0:T(8,128)(2,1)}), bf16[576,1280]{1,0:T(8,128)(2,1)}) %all-gather.2.cloned.1.call-update) | async-done | bytes 1474576 | tf_op jit(solution)/shard_map/all_gather | solution.py:128
  105.3 3.1 %add_convert_fusion = bf16[576,1024]{1,0:T(8,128)(2,1)S(1)} fusion(bf16[576,1280]{1,0:T(8,128)(2,1)} %all-gather.2.cloned.1.call-done, bf16[1280,1024]{1,0:T(8,128)(2,1)S(1)} %copy-done, f32[1024]{0:T(1024)S(1)} %copy-done.8), kind=kOutput, calls=%fused_computation.23 | convolution fusion | flops 1511129088 | bytes 5279744 | tf_op jit(solution)/shard_map/dot_general | solution.py:127
  108.4 1.1 concatenate.45
  109.5 6.0 %gather_fusion = bf16[768,1024]{1,0:T(8,128)(2,1)} fusion(bf16[577,1024]{1,0:T(8,128)(2,1)} %concatenate.45, s32[1024]{0:T(1024)S(1)} %pad_clamp_fusion), kind=kCustom, calls=%fused_computation | custom fusion | bytes 3148800 | tf_op jit(solution)/shard_map/jit(_take)/gather | solution.py:148
  115.5 1.6 %broadcast_select_fusion = bf16[4,192,1024]{2,1,0:T(8,128)(2,1)S(1)} fusion(bf16[4,192,1024]{2,1,0:T(8,128)(2,1)} %bitcast.31, pred[4,192]{1,0:T(4,128)(4,1)S(1)} %broadcast_in_dim.54), kind=kLoop, calls=%fused_computation.30 | loop fusion | flops 786432 | bytes 3146496 | tf_op jit(solution)/shard_map/jit(_take)/select_n | solution.py:148
  117.1 22.5 %all_to_all.13 = bf16[4,192,1024]{2,1,0:T(8,128)(2,1)S(1)} all-to-all(bf16[4,192,1024]{2,1,0:T(8,128)(2,1)S(1)} %broadcast_select_fusion), channel_id=1, replica_groups=mesh['seq'=4,'batch'=8] {'seq'}, dimensions={0} | all-to-all | bytes 3145728 | tf_op jit(solution)/shard_map/all_to_all | solution.py:149
  139.6 2.4 %copy.19 = bf16[192,4,1024]{2,1,0:T(4,128)(2,1)} copy(bf16[192,4,1024]{2,0,1:T(8,128)(2,1)S(1)} %bitcast.30) | data formatting | bytes 3145728 | tf_op jit(solution)/shard_map/all_to_all | solution.py:149
  142.0 3.8 %broadcast_in_dim.58 = bf16[1,192,4096]{2,1,0:T(8,128)(2,1)} reshape(bf16[192,4,1024]{2,1,0:T(4,128)(2,1)} %copy.19) | data formatting | bytes 3145728 | tf_op jit(solution)/shard_map/broadcast_in_dim | solution.py:150
  (19 shorter events, 0.1 us)
Async XLA Ops:
  6.5 98.8 %copy-start = (bf16[1280,1024]{1,0:T(8,128)(2,1)S(1)}, bf16[1280,1024]{1,0:T(8,128)(2,1)}, u32[]{:S(2)}) copy-start(bf16[1280,1024]{1,0:T(8,128)(2,1)} %param.20) | copy-start | bytes 7864324
  6.5 98.8 %all-gather.2.cloned.1.call-start = ((), (), s32[]{:S(2)}) async-start(), calls=%async_computation.1 | async-start | bytes 1843200 | tf_op jit(solution)/shard_map/all_gather | solution.py:128
  8.1 1.1 copy-start.1
  8.6 3.0 %copy-start.9 = (f32[201,128]{1,0:T(8,128)S(1)}, f32[201,128]{1,0:T(8,128)}, u32[]{:S(2)}) copy-start(f32[201,128]{1,0:T(8,128)} %constant.21.clone) | copy-start | bytes 308740
  11.7 1.3 copy-start.2
  11.7 36.0 %copy-start.6 = (f32[1280]{0:T(1024)S(1)}, f32[1280]{0:T(1024)}, u32[]{:S(2)}) copy-start(f32[1280]{0:T(1024)} %param.16) | copy-start | bytes 15364
  64.3 0.7 copy-start.7
  82.0 1.3 copy-start.3
  82.1 3.2 %copy-start.4 = (s32[1,4]{1,0:T(1,128)S(1)}, s32[1,4]{1,0:T(1,128)}, u32[]{:S(2)}) copy-start(s32[1,4]{1,0:T(1,128)} %param.13) | copy-start | bytes 52
  82.2 3.4 %copy-start.5 = (s32[1,24]{1,0:T(1,128)S(1)}, s32[1,24]{1,0:T(1,128)}, u32[]{:S(2)}) copy-start(s32[1,24]{1,0:T(1,128)} %param.14) | copy-start | bytes 292
  82.2 23.2 %copy-start.8 = (f32[1024]{0:T(1024)S(1)}, f32[1024]{0:T(1024)}, u32[]{:S(2)}) copy-start(f32[1024]{0:T(1024)} %param.21) | copy-start | bytes 12292
Sparse Core Ops, SparseCore 0:
  85.5 19.8 all-gather.1
where the time goes:
time: 153 us
  blocking collectives  57.2 us (37%)
  local copies, waits for them, and re-layouts  32.6 us (21%)
  matrix products  25.3 us (17%)
  waiting for transfers between devices  15.4 us (10%)
  between operations  13.7 us (9%)
  other arithmetic  8.41 us (5%)
    all_gather x1, blocking collectives, shards(): whole_first = lax.all_gather(conv_first, 'batch', axis=0, tiled=True)  34.7 us
    all_to_all x1, blocking collectives, shards(): lax.all_to_all(placed, 'seq', split_axis=0, concat_axis=1, tiled=True)  22.5 us
    all_gather x1, waiting for transfers between devices, shards(): lax.all_gather(token_rows, 'seq', axis=0, tiled=True)  15.4 us
    dot_general x1, matrix products, encode(): jnp.dot(second_in, conv_second, preferred_element_type=jnp.float32)  10.8 us
    dot_general x1, matrix products, encode(): jnp.dot(stacked, conv_first, preferred_element_type=jnp.float32)  7.85 us
    gather x1, local copies, waits for them, and re-layouts, shards(): placed = jnp.take(padded_rows, row_index, axis=0)  5.97 us
    reshape x1, local copies, waits for them, and re-layouts, encode(): hidden.astype(jnp.bfloat16).reshape(block_count, FRAMES // 2, 2, WIDTH)  4.31 us
    slice x1, local copies, waits for them, and re-layouts, encode(): even_rows = hidden[:, :, 0]  4.28 us
  transfers between devices with their start and end apart: 1, of which 1 were waited for; matrix products, arithmetic and copies ran while one was open for 3% of the time, Pallas kernels for 0%

commit v1 on v0

--- a/solution.py
+++ b/solution.py
@@ -12,6 +12,19 @@
 FRAMES = 96
 TOK = 24
 OWN_ROWS = 192
+
+
+def collect(value, axis, dim):
+    size, position, rows = (lax.axis_size(axis), lax.axis_index(axis), value.shape[dim])
+    right = [(i, (i + 1) % size) for i in range(size)]
+    filled = jnp.zeros((*value.shape[:dim], size * rows, *value.shape[dim + 1 :]), value.dtype)
+    carried = value
+    for lap in range(size):
+        owner = (position - lap) % size
+        filled = lax.dynamic_update_slice_in_dim(filled, carried, owner * rows, axis=dim)
+        if lap < size - 1:
+            carried = lax.ppermute(carried, axis, right)
+    return filled
 
 
 def hertz_to_mel(hertz):
@@ -116,7 +129,7 @@
     slots_all = waveforms.shape[1]
     lengths = clip_lengths[0]
     starts = block_starts[0]
-    whole_first = lax.all_gather(conv_first, "batch", axis=0, tiled=True)
+    whole_first = collect(conv_first, "batch", 0)
     blocks = waveforms[0]
     group_slot = jnp.arange(devices_seq * slots_all, dtype=jnp.int32)
     group_live = group_slot % slots_all < jnp.repeat(lengths, slots_all)

time: 153 us -> 169 us (1.10)
  waiting for transfers between devices: 15.4 us -> 52.1 us
  blocking collectives: 57.2 us -> 22.5 us
  local copies, waits for them, and re-layouts: 32.6 us -> 40.5 us
  starting transfers between devices: 0.01 us -> 4.58 us
    ppermute x0 -> x7, waiting for transfers between devices: none -> 40.1 us  [collect(): carried = lax.ppermute(carried, axis, right)]
    all_gather x1 -> x0, blocking collectives: 34.7 us -> none  [shards(): whole_first = lax.all_gather(conv_first, 'batch', axis=0, tiled=True)]
    dynamic_update_slice x0 -> x8, local copies, waits for them, and re-layouts: none -> 6.56 us  [collect(): lax.dynamic_update_slice_in_dim(filled, carried, owner * rows, axis=dim)]
    ppermute x0 -> x7, starting transfers between devices: none -> 4.58 us  [collect(): carried = lax.ppermute(carried, axis, right)]
    all_gather x1, waiting for transfers between devices: 15.4 us -> 11.9 us  [shards(): lax.all_gather(token_rows, 'seq', axis=0, tiled=True)]
  transfers between devices with their start and end apart: 1 -> 8, of which waited for: 1 -> 7; matrix products, arithmetic and copies ran while one was open for 3% -> 10% of each run, Pallas kernels for 0% -> 0%
where the time goes in v1:
time: 169 us; the launch traced here: 168 us
  waiting for transfers between devices  52.1 us (31%)
  local copies, waits for them, and re-layouts  40.5 us (24%)
  matrix products  26.5 us (16%)
  blocking collectives  22.5 us (13%)
  between operations  13.8 us (8%)
  other arithmetic  8.41 us (5%)
  starting transfers between devices  4.58 us (3%)
    ppermute x7, waiting for transfers between devices, collect(): carried = lax.ppermute(carried, axis, right)  40.1 us
    all_to_all x1, blocking collectives, shards(): lax.all_to_all(placed, 'seq', split_axis=0, concat_axis=1, tiled=True)  22.5 us
    all_gather x1, waiting for transfers between devices, shards(): lax.all_gather(token_rows, 'seq', axis=0, tiled=True)  11.9 us
    dot_general x1, matrix products, encode(): jnp.dot(second_in, conv_second, preferred_element_type=jnp.float32)  10.8 us
    dot_general x1, matrix products, encode(): jnp.dot(stacked, conv_first, preferred_element_type=jnp.float32)  9.05 us
    dynamic_update_slice x8, local copies, waits for them, and re-layouts, collect(): lax.dynamic_update_slice_in_dim(filled, carried, owner * rows, axis=dim)  6.56 us
    gather x1, local copies, waits for them, and re-layouts, shards(): placed = jnp.take(padded_rows, row_index, axis=0)  5.97 us
    ppermute x7, starting transfers between devices, collect(): carried = lax.ppermute(carried, axis, right)  4.58 us
  transfers between devices with their start and end apart: 8, of which 7 were waited for; matrix products, arithmetic and copies ran while one was open for 10% of the time, Pallas kernels for 0%

profile of v1, /device:TPU:0, one launch (start us, length us, event | category | flops | bytes accessed | tf_op | source)
XLA Modules:
  0.0 168.5 jit_solution(12439483199741570245)
XLA Ops:
  6.5 3.0 %collective-permute-start = (bf16[48,1280]{1,0:T(8,128)(2,1)}, bf16[48,1280]{1,0:T(8,128)(2,1)}, u32[]{:S(2)}, u32[]{:S(2)}) collective-permute-start(bf16[48,1280]{1,0:T(8,128)(2,1)} %param.15), channel_id=1, source_target_pairs={{0,1},{1,2},{2,3},{3,4},{4,5},{5,6},{6,7},{7,0},{8,9},{9,10},{10,1... | collective-permute-start | bytes 368648 | tf_op jit(solution)/shard_map/ppermute | solution.py:26
  9.5 1.3 reshape.141
  10.8 1.1 fusion.49
  12.1 1.0 constant_dynamic-update-slice_fusion.7
  13.2 0.9 copy-done.3
  14.1 0.5 pad_maximum_fusion
  14.6 2.4 %fusion.50 = f32[576,402]{0,1:T(8,128)S(1)} fusion(f32[576,400]{1,0:T(8,128)S(1)} %bitcast.32, f32[400,402]{1,0:T(8,128)S(1)} %copy-done.4), kind=kOutput, calls=%fused_computation.96 | convolution fusion | flops 1111449600 | bytes 2491008 | tf_op jit(solution)/shard_map/dot_general | solution.py:77
  17.0 1.2 fusion.30
  18.4 1.6 collective-permute-start.1
  20.0 1.6 constant_dynamic-update-slice_fusion.6
  21.6 4.6 %collective-permute-done.1 = bf16[48,1280]{1,0:T(8,128)(2,1)S(1)} collective-permute-done((bf16[48,1280]{1,0:T(8,128)(2,1)}, bf16[48,1280]{1,0:T(8,128)(2,1)S(1)}, u32[]{:S(2)}, u32[]{:S(2)}) %collective-permute-start.1) | collective-permute-done | bytes 122912 | tf_op jit(solution)/shard_map/ppermute | solution.py:26
  26.3 0.7 constant_dynamic-update-slice_fusion.5
  26.9 6.9 %collective-permute-done.2 = bf16[48,1280]{1,0:T(8,128)(2,1)S(1)} collective-permute-done((bf16[48,1280]{1,0:T(8,128)(2,1)S(1)}, bf16[48,1280]{1,0:T(8,128)(2,1)S(1)}, u32[]{:S(2)}, u32[]{:S(2)}) %collective-permute-start.2) | collective-permute-done | bytes 122912 | tf_op jit(solution)/shard_map/ppermute | solution.py:26
  33.8 0.7 constant_dynamic-update-slice_fusion.4
  34.5 6.9 %collective-permute-done.3 = bf16[48,1280]{1,0:T(8,128)(2,1)S(1)} collective-permute-done((bf16[48,1280]{1,0:T(8,128)(2,1)S(1)}, bf16[48,1280]{1,0:T(8,128)(2,1)S(1)}, u32[]{:S(2)}, u32[]{:S(2)}) %collective-permute-start.3) | collective-permute-done | bytes 122912 | tf_op jit(solution)/shard_map/ppermute | solution.py:26
  41.4 0.7 constant_dynamic-update-slice_fusion.3
  42.1 6.9 %collective-permute-done.4 = bf16[48,1280]{1,0:T(8,128)(2,1)S(1)} collective-permute-done((bf16[48,1280]{1,0:T(8,128)(2,1)S(1)}, bf16[48,1280]{1,0:T(8,128)(2,1)S(1)}, u32[]{:S(2)}, u32[]{:S(2)}) %collective-permute-start.4) | collective-permute-done | bytes 122912 | tf_op jit(solution)/shard_map/ppermute | solution.py:26
  49.0 0.6 constant_dynamic-update-slice_fusion.2
  49.6 7.8 %collective-permute-done.5 = bf16[48,1280]{1,0:T(8,128)(2,1)S(1)} collective-permute-done((bf16[48,1280]{1,0:T(8,128)(2,1)S(1)}, bf16[48,1280]{1,0:T(8,128)(2,1)S(1)}, u32[]{:S(2)}, u32[]{:S(2)}) %collective-permute-start.5) | collective-permute-done | bytes 122912 | tf_op jit(solution)/shard_map/ppermute | solution.py:26
  57.5 0.7 constant_dynamic-update-slice_fusion.1
  58.1 6.9 %collective-permute-done.6 = bf16[48,1280]{1,0:T(8,128)(2,1)S(1)} collective-permute-done((bf16[48,1280]{1,0:T(8,128)(2,1)S(1)}, bf16[48,1280]{1,0:T(8,128)(2,1)S(1)}, u32[]{:S(2)}, u32[]{:S(2)}) %collective-permute-start.6) | collective-permute-done | bytes 122912 | tf_op jit(solution)/shard_map/ppermute | solution.py:26
  65.0 0.7 constant_dynamic-update-slice_fusion
  65.7 9.1 %fusion.2 = bf16[576,1280]{1,0:T(8,128)(2,1)} fusion(bf16[384,1280]{1,0:T(8,128)(2,1)} %constant_dynamic-update-slice_fusion, f32[1280]{0:T(1024)S(1)} %copy-done.8, bf16[576,128]{1,0:T(8,128)(2,1)S(1)} %bitcast.39, bf16[576,128]{1,0:T(8,128)(2,1)S(1)} %fusion.30, bf16[576,128]{1,0:T(8,128)(2,1)S(1)} %bitcast.38), kind=kOutput, calls=%fused_computation.6 | convolution fusion | flops 616218624 | bytes 2905088 | tf_op jit(solution)/shard_map/dot_general | solution.py:91
  74.8 4.3 %reshape.139 = bf16[6,48,2,1280]{3,2,1,0:T(2,128)(2,1)} reshape(bf16[576,1280]{1,0:T(8,128)(2,1)} %fusion.2) | data formatting | bytes 2949120 | tf_op jit(solution)/shard_map/reshape | solution.py:94
  79.1 4.3 %fusion.48 = (bf16[6,48,1,1280]{3,2,1,0:T(2,128)(2,1)S(1)}, bf16[6,48,1,1280]{3,2,1,0:T(2,128)(2,1)S(1)}) fusion(bf16[6,48,2,1280]{3,2,1,0:T(2,128)(2,1)} %reshape.139), kind=kLoop, calls=%fused_computation.94 | loop fusion | bytes 2949120 | tf_op jit(solution)/shard_map/slice | solution.py:95
  83.4 0.1 copy.23
  83.5 0.1 copy.20
  83.6 0.2 concatenate.40
  83.9 0.4 copy-done.9
  84.3 10.8 %fusion.16 = f32[288,1280]{1,0:T(8,128)} fusion(bf16[3840,1280]{1,0:T(8,128)(2,1)} %param.17, bf16[288,1280]{1,0:T(8,128)(2,1)S(1)} %bitcast.34, bf16[288,1280]{1,0:T(8,128)(2,1)S(1)} %bitcast.36, bf16[288,1280]{1,0:T(8,128)(2,1)S(1)} %bitcast.35, f32[1280]{0:T(1024)S(1)} %copy-done.9), kind=kOutput, calls=%fused_computation.32 | convolution fusion | flops 2861752320 | bytes 13521920 | tf_op jit(solution)/shard_map/dot_general | solution.py:104
  95.1 3.0 %reshape.140 = f32[6,24,2,1280]{3,2,1,0:T(2,128)} reshape(f32[288,1280]{1,0:T(8,128)} %fusion.16) | data formatting | bytes 2949120 | tf_op jit(solution)/shard_map/reshape | solution.py:107
  98.1 3.1 %reduce_sum.27 = f32[6,24,1280]{2,1,0:T(8,128)S(1)} reduce(f32[6,24,2,1280]{3,2,1,0:T(2,128)} %reshape.140, f32[]{:T(128)} %constant.95.clone.1), dimensions={2}, to_apply=%region_1.2 | reduce | flops 184320 | bytes 2211844 | tf_op jit(solution)/shard_map/reduce_sum | solution.py:107
  101.3 0.1 fusion.47
  101.4 0.9 multiply_reduce_fusion
  102.5 0.1 sqrt.12
  102.5 2.0 %fusion.33 = bf16[144,1280]{1,0:T(8,128)(2,1)} fusion(f32[6,24,1280]{2,1,0:T(8,128)} %get-tuple-element.8, f32[1280]{0:T(1024)S(1)} %copy-done.5, f32[144]{0:T(256)S(1)} %sqrt.12, f32[144]{0:T(256)S(1)} %div.33), kind=kLoop, calls=%fused_computation.58 | loop fusion | flops 737280 | bytes 1112192 | tf_op jit(solution)/shard_map/convert_element_type | solution.py:112
  104.7 0.1 reshape.136
  104.9 0.1 select_n.106
  105.0 4.1 %scatter_custom_fusion = s32[768]{0:T(1024)S(1)} fusion(s32[576]{0:T(1024)S(1)} %fusion.41, s32[576]{0:T(1024)S(1)} %iota.13, s32[]{:T(128)} %constant.61.clone.1), kind=kCustom, calls=%fused_computation.87 | custom fusion | bytes 3076 | tf_op jit(solution)/shard_map/scatter | solution.py:156
  109.1 0.1 broadcast_in_dim.57
  109.2 11.9 %all-gather.2.cloned.1.call-done = bf16[576,1280]{1,0:T(8,128)(2,1)} async-done(((bf16[144,1280]{1,0:T(8,128)(2,1)}), bf16[576,1280]{1,0:T(8,128)(2,1)}) %all-gather.2.cloned.1.call-update) | async-done | bytes 1474576 | tf_op jit(solution)/shard_map/all_gather | solution.py:141
  121.1 3.1 %add_convert_fusion = bf16[576,1024]{1,0:T(8,128)(2,1)S(1)} fusion(bf16[576,1280]{1,0:T(8,128)(2,1)} %all-gather.2.cloned.1.call-done, bf16[1280,1024]{1,0:T(8,128)(2,1)S(1)} %copy-done, f32[1024]{0:T(1024)S(1)} %copy-done.10), kind=kOutput, calls=%fused_computation.23 | convolution fusion | flops 1511129088 | bytes 5279744 | tf_op jit(solution)/shard_map/dot_general | solution.py:140
  124.2 1.1 concatenate.45
  125.3 6.0 %gather_fusion = bf16[768,1024]{1,0:T(8,128)(2,1)} fusion(bf16[577,1024]{1,0:T(8,128)(2,1)} %concatenate.45, s32[1024]{0:T(1024)S(1)} %pad_clamp_fusion), kind=kCustom, calls=%fused_computation | custom fusion | bytes 3148800 | tf_op jit(solution)/shard_map/jit(_take)/gather | solution.py:161
  131.3 1.6 broadcast_select_fusion
  132.9 22.5 %all_to_all.13 = bf16[4,192,1024]{2,1,0:T(8,128)(2,1)S(1)} all-to-all(bf16[4,192,1024]{2,1,0:T(8,128)(2,1)S(1)} %broadcast_select_fusion), channel_id=1, replica_groups=mesh['seq'=4,'batch'=8] {'seq'}, dimensions={0} | all-to-all | bytes 3145728 | tf_op jit(solution)/shard_map/all_to_all | solution.py:162
  155.4 2.4 %copy.19 = bf16[192,4,1024]{2,1,0:T(4,128)(2,1)} copy(bf16[192,4,1024]{2,0,1:T(8,128)(2,1)S(1)} %bitcast.30) | data formatting | bytes 3145728 | tf_op jit(solution)/shard_map/all_to_all | solution.py:162
  157.8 3.8 %broadcast_in_dim.62 = bf16[1,192,4096]{2,1,0:T(8,128)(2,1)} reshape(bf16[192,4,1024]{2,1,0:T(4,128)(2,1)} %copy.19) | data formatting | bytes 3145728 | tf_op jit(solution)/shard_map/broadcast_in_dim | solution.py:163
  (45 shorter events, 0.6 us)
Async XLA Ops:
  6.5 114.6 %copy-start = (bf16[1280,1024]{1,0:T(8,128)(2,1)S(1)}, bf16[1280,1024]{1,0:T(8,128)(2,1)}, u32[]{:S(2)}) copy-start(bf16[1280,1024]{1,0:T(8,128)(2,1)} %param.20) | copy-start | bytes 7864324
  6.5 114.6 %all-gather.2.cloned.1.call-start = ((), (), s32[]{:S(2)}) async-start(), calls=%async_computation.1 | async-start | bytes 1843200 | tf_op jit(solution)/shard_map/all_gather | solution.py:141
  6.5 11.9 %collective-permute-start = (bf16[48,1280]{1,0:T(8,128)(2,1)}, bf16[48,1280]{1,0:T(8,128)(2,1)}, u32[]{:S(2)}, u32[]{:S(2)}) collective-permute-start(bf16[48,1280]{1,0:T(8,128)(2,1)} %param.15), channel_id=1, source_target_pairs={{0,1},{1,2},{2,3},{3,4},{4,5},{5,6},{6,7},{7,0},{8,9},{9,10},{10,1... | collective-permute-start | bytes 368648 | tf_op jit(solution)/shard_map/ppermute | solution.py:26
  12.0 2.1 %copy-start.1 = (f32[6,96,160]{2,1,0:T(8,128)S(1)}, f32[6,96,160]{2,1,0:T(8,128)}, u32[]{:S(2)}) copy-start(f32[6,96,160]{2,1,0:T(8,128)} %get-tuple-element.9) | copy-start | bytes 1105924
  12.0 2.1 %copy-start.2 = (f32[6,96,160]{2,1,0:T(8,128)S(1)}, f32[6,96,160]{2,1,0:T(8,128)}, u32[]{:S(2)}) copy-start(f32[6,96,160]{2,1,0:T(8,128)} %get-tuple-element.10) | copy-start | bytes 1105924
  12.1 2.5 %copy-start.4 = (f32[400,402]{1,0:T(8,128)S(1)}, f32[400,402]{1,0:T(8,128)}, u32[]{:S(2)}) copy-start(f32[400,402]{1,0:T(8,128)} %constant.217.clone) | copy-start | bytes 1929604
  13.1 1.0 copy-start.3
  14.6 2.4 %copy-start.11 = (f32[201,128]{1,0:T(8,128)S(1)}, f32[201,128]{1,0:T(8,128)}, u32[]{:S(2)}) copy-start(f32[201,128]{1,0:T(8,128)} %constant.218.clone) | copy-start | bytes 308740
  17.0 48.7 %copy-start.8 = (f32[1280]{0:T(1024)S(1)}, f32[1280]{0:T(1024)}, u32[]{:S(2)}) copy-start(f32[1280]{0:T(1024)} %param.16) | copy-start | bytes 15364
  18.4 7.8 %collective-permute-start.1 = (bf16[48,1280]{1,0:T(8,128)(2,1)}, bf16[48,1280]{1,0:T(8,128)(2,1)S(1)}, u32[]{:S(2)}, u32[]{:S(2)}) collective-permute-start(bf16[48,1280]{1,0:T(8,128)(2,1)} %collective-permute-done), channel_id=1, source_target_pairs={{0,1},{1,2},{2,3},{3,4},{4,5},{5,6},{6,7},{7,0},{8,9},{9,10},{10,1... | collective-permute-start | bytes 368648 | tf_op jit(solution)/shard_map/ppermute | solution.py:26
  26.3 7.6 %collective-permute-start.2 = (bf16[48,1280]{1,0:T(8,128)(2,1)S(1)}, bf16[48,1280]{1,0:T(8,128)(2,1)S(1)}, u32[]{:S(2)}, u32[]{:S(2)}) collective-permute-start(bf16[48,1280]{1,0:T(8,128)(2,1)S(1)} %collective-permute-done.1), channel_id=1, source_target_pairs={{0,1},{1,2},{2,3},{3,4},{4,5},{5,6},{6,7},{7,0},{8,9},{9,10},{10,1... | collective-permute-start | bytes 368648 | tf_op jit(solution)/shard_map/ppermute | solution.py:26
  33.8 7.6 %collective-permute-start.3 = (bf16[48,1280]{1,0:T(8,128)(2,1)S(1)}, bf16[48,1280]{1,0:T(8,128)(2,1)S(1)}, u32[]{:S(2)}, u32[]{:S(2)}) collective-permute-start(bf16[48,1280]{1,0:T(8,128)(2,1)S(1)} %collective-permute-done.2), channel_id=1, source_target_pairs={{0,1},{1,2},{2,3},{3,4},{4,5},{5,6},{6,7},{7,0},{8,9},{9,10},{10,1... | collective-permute-start | bytes 368648 | tf_op jit(solution)/shard_map/ppermute | solution.py:26
  41.4 7.6 %collective-permute-start.4 = (bf16[48,1280]{1,0:T(8,128)(2,1)S(1)}, bf16[48,1280]{1,0:T(8,128)(2,1)S(1)}, u32[]{:S(2)}, u32[]{:S(2)}) collective-permute-start(bf16[48,1280]{1,0:T(8,128)(2,1)S(1)} %collective-permute-done.3), channel_id=1, source_target_pairs={{0,1},{1,2},{2,3},{3,4},{4,5},{5,6},{6,7},{7,0},{8,9},{9,10},{10,1... | collective-permute-start | bytes 368648 | tf_op jit(solution)/shard_map/ppermute | solution.py:26
  49.0 8.5 %collective-permute-start.5 = (bf16[48,1280]{1,0:T(8,128)(2,1)S(1)}, bf16[48,1280]{1,0:T(8,128)(2,1)S(1)}, u32[]{:S(2)}, u32[]{:S(2)}) collective-permute-start(bf16[48,1280]{1,0:T(8,128)(2,1)S(1)} %collective-permute-done.4), channel_id=1, source_target_pairs={{0,1},{1,2},{2,3},{3,4},{4,5},{5,6},{6,7},{7,0},{8,9},{9,10},{10,1... | collective-permute-start | bytes 368648 | tf_op jit(solution)/shard_map/ppermute | solution.py:26
  57.5 7.6 %collective-permute-start.6 = (bf16[48,1280]{1,0:T(8,128)(2,1)S(1)}, bf16[48,1280]{1,0:T(8,128)(2,1)S(1)}, u32[]{:S(2)}, u32[]{:S(2)}) collective-permute-start(bf16[48,1280]{1,0:T(8,128)(2,1)S(1)} %collective-permute-done.5), channel_id=1, source_target_pairs={{0,1},{1,2},{2,3},{3,4},{4,5},{5,6},{6,7},{7,0},{8,9},{9,10},{10,1... | collective-permute-start | bytes 368648 | tf_op jit(solution)/shard_map/ppermute | solution.py:26
  83.6 0.7 copy-start.9
  101.3 1.3 copy-start.5
  101.4 3.2 %copy-start.6 = (s32[1,4]{1,0:T(1,128)S(1)}, s32[1,4]{1,0:T(1,128)}, u32[]{:S(2)}) copy-start(s32[1,4]{1,0:T(1,128)} %param.13) | copy-start | bytes 52
  101.4 3.4 %copy-start.7 = (s32[1,24]{1,0:T(1,128)S(1)}, s32[1,24]{1,0:T(1,128)}, u32[]{:S(2)}) copy-start(s32[1,24]{1,0:T(1,128)} %param.14) | copy-start | bytes 292
  101.4 19.7 %copy-start.10 = (f32[1024]{0:T(1024)S(1)}, f32[1024]{0:T(1024)}, u32[]{:S(2)}) copy-start(f32[1024]{0:T(1024)} %param.21) | copy-start | bytes 12292
Sparse Core Ops, SparseCore 0:
  104.7 16.3 all-gather.1
